TPU v7x, 256 devices: a whole 4x4x8 slice. The times are simulated.
256 devices in a mesh: seq: 16 (over z, core), mp: 8 (over y, x_hi), dp: 2 (over x_lo).
Axes of the slice: x: 4 (x_hi: 2, x_lo: 2; x = x_hi * 2 + x_lo), y: 4, z: 8, core: 2. Of those that a mesh axis runs over, the one named last changes fastest.
Arguments:
- latents: bfloat16 [2, 3072, 1792], P('dp', 'seq', 'mp'), may hold values from -6 to 6
- grad_out: bfloat16 [2, 3072, 1792], P('dp', 'seq', 'mp'), may hold values from -6 to 6
- sync_mod: bfloat16 [2, 2400, 3584], P('dp', 'seq'), may hold values from -3 to 3
- w_qkv: bfloat16 [1792, 3, 1024], P(None, None, 'mp'), may hold values from -0.125 to 0.125
- w_out: bfloat16 [1024, 1792], P('mp'), may hold values from -0.1875 to 0.1875
- q_gain: float32 [8, 128], P('mp'), may hold values from 0.5 to 2.5
- k_gain: float32 [8, 128], P('mp'), may hold values from 0.5 to 2.5
- frame_of: int32 [2, 3072], P('dp', 'seq'), may hold values from 0 to 2399, as said below
- group_id: int32 [2, 3072], P('dp'), may hold values from 0 to 63, never falling along the last dimension, each value on 1 to 96 neighbouring positions
- clip_len: int32 [2], P('dp'), may hold values from 1536 to 3072
Outputs:
- mixed: bfloat16 [2, 3072, 1792], P('dp', 'seq', 'mp')
- grad_latents: bfloat16 [2, 3072, 1792], P('dp', 'seq', 'mp')
- grad_wqkv: float32 [1792, 3, 1024], P(('seq', 'dp'), None, 'mp')
- grad_wout: float32 [1024, 1792], P('mp', ('seq', 'dp'))
Inputs may be any that keep to these rules, and one draw needn't show every extreme that they name: frame_of[c, l] = floor((96 l + s) / 125) with a phase s of 0 to 124 drawn for each clip, so the latents on seq index j read frames held by seq indices j - 1 and j only.
All inputs are finite; a program needn't handle non-finite values.
Results may differ from a plain program's by a relative error of at most 0.012.
The roundings to bfloat16 on the way count: a program that leaves them out, or rounds other values in their place, can miss the bound.
Values may be sent and summed in bfloat16 or wider, within the bound.
A program may use at most 64 MiB of HBM per device.

v0:
```python
import jax
import jax.numpy as jnp
from jax import lax
from jax.sharding import PartitionSpec as P

EPSILON = 1e-06
NEG_FILL = -1e30


def from_behind(value, axis, steps):
    count = lax.axis_size(axis)
    leading, last = (max(0, -steps), min(count, count - steps))
    return lax.ppermute(value, axis, [(source, source + steps) for source in range(leading, last)])


def inv_rms(values):
    return lax.rsqrt(jnp.mean(values * values, axis=-1, keepdims=True) + EPSILON)


def norm_back(raw, inv_norm, gains, upstream):
    inner_dot = jnp.mean(upstream * gains * raw, axis=-1, keepdims=True)
    return inv_norm * (gains * upstream - raw * inv_norm * inv_norm * inner_dot)


def group_mask(group_ids, clip_length, query_first, query_span, key_span):
    query_group = lax.dynamic_slice_in_dim(group_ids, query_first, query_span, 1)
    key_place = lax.iota(jnp.int32, key_span)
    allowed = (group_ids[:, None, :] <= query_group[:, :, None]) & (
        key_place[None, None, :] < clip_length[:, None, None]
    )
    return allowed[:, None, :, :]


def head_logits(queries, keys, factor):
    return jnp.einsum("cqhd,ckhd->chqk", queries, keys, preferred_element_type=jnp.float32) * factor


def on_device(
    latents, grad_out, sync_mod, w_qkv, w_out, q_gain, k_gain, frame_of, group_id, clip_len
):
    clip_count, row_count, width_part = latents.shape
    frame_count = sync_mod.shape[1]
    model_width = sync_mod.shape[2] // 2
    heads_here, head_dim = q_gain.shape
    inner_width = heads_here * head_dim
    factor = head_dim ** (-0.5)
    seq_place = lax.axis_index("seq")
    model_place = lax.axis_index("mp")
    query_first = seq_place * row_count
    inputs_full, upstream_full = (
        lax.all_gather(latents, "mp", axis=2, tiled=True),
        lax.all_gather(grad_out, "mp", axis=2, tiled=True),
    )
    earlier = from_behind(sync_mod, "seq", 1)
    window = jnp.concatenate([earlier, sync_mod], axis=1)
    local_frame = frame_of - (seq_place * frame_count - frame_count)
    selector = (
        local_frame[:, :, None] == lax.iota(jnp.int32, 2 * frame_count)[None, None, :]
    ).astype(jnp.bfloat16)
    modulation = jnp.einsum("clf,cfe->cle", selector, window, preferred_element_type=jnp.float32)
    mod_scale = modulation[:, :, :model_width]
    mod_gate = modulation[:, :, model_width:]
    inputs_f = inputs_full.astype(jnp.float32)
    inv_norm = inv_rms(inputs_f)
    normed = inputs_f * inv_norm
    hidden = (normed * (1.0 + mod_scale)).astype(jnp.bfloat16)
    flat_hidden = hidden.reshape(clip_count * row_count, model_width)
    flat_weight = w_qkv.reshape(model_width, 3 * inner_width)
    projected = jnp.dot(flat_hidden, flat_weight, preferred_element_type=jnp.float32)
    projected = projected.reshape(clip_count, row_count, 3, heads_here, head_dim)
    query_raw = projected[:, :, 0]
    key_raw = projected[:, :, 1]
    query_inv = inv_rms(query_raw)
    key_inv = inv_rms(key_raw)
    query_norm = (query_raw * query_inv * q_gain).astype(jnp.bfloat16)
    key_norm = (key_raw * key_inv * k_gain).astype(jnp.bfloat16)
    values = projected[:, :, 2].astype(jnp.bfloat16)
    row_max = jnp.full((clip_count, heads_here, row_count), NEG_FILL, jnp.float32)
    key_piece = lax.all_gather(key_norm, "seq", axis=1, tiled=True)
    value_piece = lax.all_gather(values, "seq", axis=1, tiled=True)
    span_len = key_piece.shape[1]
    allowed = group_mask(group_id, clip_len, query_first, row_count, span_len)
    logits = jnp.where(allowed, head_logits(query_norm, key_piece, factor), NEG_FILL)
    new_max = jnp.maximum(row_max, jnp.max(logits, axis=-1))
    unnorm = jnp.where(allowed, jnp.exp(logits - new_max[..., None]), 0.0)
    row_sum = jnp.sum(unnorm, axis=-1)
    row_acc = jnp.einsum(
        "chqk,ckhd->chqd",
        unnorm.astype(jnp.bfloat16),
        value_piece,
        preferred_element_type=jnp.float32,
    )
    row_max, row_sum, row_acc = (new_max, row_sum, row_acc)
    key_all, value_all = (
        lax.all_gather(key_norm, "seq", axis=1, tiled=True),
        lax.all_gather(values, "seq", axis=1, tiled=True),
    )
    heads_out = jnp.transpose(row_acc / row_sum[..., None], (0, 2, 1, 3)).astype(jnp.bfloat16)
    out_rows = heads_out.reshape(clip_count * row_count, inner_width)
    attn_part = jnp.dot(out_rows, w_out, preferred_element_type=jnp.float32).reshape(
        clip_count, row_count, model_width
    )
    attn_mine = lax.psum_scatter(attn_part, "mp", scatter_dimension=2, tiled=True)
    gate_mine = lax.dynamic_slice_in_dim(mod_gate, model_place * width_part, width_part, 2)
    mixed = (latents.astype(jnp.float32) + gate_mine * attn_mine).astype(jnp.bfloat16)
    grad_attn = (upstream_full.astype(jnp.float32) * mod_gate).astype(jnp.bfloat16)
    flat_grad = grad_attn.reshape(clip_count * row_count, model_width)
    grad_wout = jnp.einsum("ti,td->id", out_rows, flat_grad, preferred_element_type=jnp.float32)
    grad_heads = jnp.einsum(
        "td,id->ti", flat_grad, w_out, preferred_element_type=jnp.float32
    ).astype(jnp.bfloat16)
    grad_heads = grad_heads.reshape(clip_count, row_count, heads_here, head_dim)
    out_dot = jnp.transpose(
        jnp.sum(grad_heads.astype(jnp.float32) * heads_out.astype(jnp.float32), axis=-1), (0, 2, 1)
    )
    allowed_all = group_mask(group_id, clip_len, query_first, row_count, key_all.shape[1])
    logits_all = head_logits(query_norm, key_all, factor)
    probs = jnp.where(
        allowed_all, jnp.exp(logits_all - row_max[..., None]) / row_sum[..., None], 0.0
    )
    grad_probs = jnp.einsum(
        "cqhd,ckhd->chqk", grad_heads, value_all, preferred_element_type=jnp.float32
    )
    grad_logits = (probs * (grad_probs - out_dot[..., None])).astype(jnp.bfloat16)
    grad_qnorm = (
        jnp.einsum("chqk,ckhd->cqhd", grad_logits, key_all, preferred_element_type=jnp.float32)
        * factor
    )
    grad_key_all = (
        jnp.einsum("chqk,cqhd->ckhd", grad_logits, query_norm, preferred_element_type=jnp.float32)
        * factor
    )
    grad_value_all = jnp.einsum(
        "chqk,cqhd->ckhd",
        probs.astype(jnp.bfloat16),
        grad_heads,
        preferred_element_type=jnp.float32,
    )
    key_terms = jnp.stack([grad_key_all, grad_value_all], axis=2)
    key_share = lax.psum_scatter(key_terms, "seq", scatter_dimension=1, tiled=True)
    grad_knorm = key_share[:, :, 0]
    grad_values = key_share[:, :, 1]
    grad_query = norm_back(query_raw, query_inv, q_gain, grad_qnorm)
    grad_key = norm_back(key_raw, key_inv, k_gain, grad_knorm)
    grad_proj = jnp.stack([grad_query, grad_key, grad_values], axis=2).astype(jnp.bfloat16)
    grad_proj = grad_proj.reshape(clip_count * row_count, 3 * inner_width)
    grad_wqkv = jnp.einsum(
        "te,tf->ef", flat_hidden, grad_proj, preferred_element_type=jnp.float32
    ).reshape(model_width, 3, inner_width)
    grad_wqkv, grad_wout = (
        lax.psum_scatter(grad_wqkv, ("seq", "dp"), scatter_dimension=0, tiled=True),
        lax.psum_scatter(grad_wout, ("seq", "dp"), scatter_dimension=1, tiled=True),
    )
    grad_hidden = jnp.einsum(
        "tf,ef->te", grad_proj, flat_weight, preferred_element_type=jnp.float32
    )
    grad_hidden = grad_hidden.reshape(clip_count, row_count, model_width)
    grad_full = lax.psum(grad_hidden, "mp")
    grad_normed = grad_full * (1.0 + mod_scale)
    grad_whole = inv_norm * (
        grad_normed - normed * jnp.mean(grad_normed * normed, axis=-1, keepdims=True)
    )
    grad_inputs = lax.dynamic_slice_in_dim(grad_whole, model_place * width_part, width_part, 2)
    grad_latents = (grad_out.astype(jnp.float32) + grad_inputs).astype(jnp.bfloat16)
    return (mixed, grad_latents, grad_wqkv, grad_wout)


def solution(mesh):
    in_specs = (
        P("dp", "seq", "mp"),
        P("dp", "seq", "mp"),
        P("dp", "seq", None),
        P(None, None, "mp"),
        P("mp", None),
        P("mp", None),
        P("mp", None),
        P("dp", "seq"),
        P("dp", None),
        P("dp"),
    )
    out_specs = (
        P("dp", "seq", "mp"),
        P("dp", "seq", "mp"),
        P(("seq", "dp"), None, "mp"),
        P("mp", ("seq", "dp")),
    )
    return jax.shard_map(
        on_device, mesh=mesh, in_specs=in_specs, out_specs=out_specs, check_vma=False
    )
```

profile of v0, /device:TPU:1, one launch (start us, length us, event | category | flops | bytes accessed | tf_op | source)
XLA Modules:
  0.0 658.3 jit_solution(18341032263958154900)
XLA Ops:
  7.2 0.0 copy-start
  7.2 0.0 reduce-scatter.10.cloned.1.call-start
  7.2 5.1 collective-permute-start
  12.9 1.1 copy.23
  14.0 1.1 copy.27
  15.1 2.6 copy.25
  17.7 41.4 %all_gather.17 = bf16[1,192,1792]{1,0,2:T(2,128)(2,1)S(1)} all-gather(bf16[1,192,224]{1,0,2:T(2,128)(2,1)S(1)} %copy.27), channel_id=1, replica_groups=mesh['seq'=16,'mp'=8,'dp'=2] {'mp'}, dimensions={2}, use_global_device_ids=true | all-gather | bytes 774144 | tf_op jit(solution)/shard_map/all_gather | solution.py:52
  59.0 3.8 copy.28
  62.9 38.2 %all_gather.14 = bf16[1,192,1792]{1,0,2:T(2,128)(2,1)S(1)} all-gather(bf16[1,192,224]{1,0,2:T(2,128)(2,1)S(1)} %copy.23), channel_id=1, replica_groups=mesh['seq'=16,'mp'=8,'dp'=2] {'mp'}, dimensions={2}, use_global_device_ids=true | all-gather | bytes 774144 | tf_op jit(solution)/shard_map/all_gather | solution.py:51
  101.1 4.0 copy.24
  105.0 0.1 constant_dynamic-slice_fusion
  105.1 0.2 fusion.7
  105.4 0.5 copy-done.2
  105.9 2.6 convolution_bitcast_fusion
  108.5 1.4 convert_multiply_fusion
  109.9 0.2 copy-done.1
  110.0 0.6 fusion.8
  110.6 0.1 fusion.45
  110.8 0.0 copy-start.17
  110.8 0.1 fusion.48
  110.9 28.8 %all-gather = bf16[1,3072,1,1,128]{4,1,2,3,0:T(8,128)(2,1)S(1)} all-gather(bf16[1,192,1,1,128]{4,1,2,3,0:T(8,128)(2,1)S(1)} %slice.67), channel_id=2, replica_groups=mesh['seq'=16,'mp'=8,'dp'=2] {'seq'}, dimensions={1}, use_global_device_ids=true | all-gather | bytes 835584 | tf_op jit(solution)/shard_map/all_gather | solution.py:80
  139.7 0.1 fusion.47
  139.8 17.0 %all_gather.15 = bf16[1,3072,1,128]{3,1,2,0:T(8,128)(2,1)S(1)} all-gather(bf16[1,192,1,128]{3,1,2,0:T(8,128)(2,1)S(1)} %fusion.47), channel_id=1, replica_groups=mesh['seq'=16,'mp'=8,'dp'=2] {'seq'}, dimensions={1}, use_global_device_ids=true | all-gather | bytes 835584 | tf_op jit(solution)/shard_map/all_gather | solution.py:79
  156.8 0.8 fusion.6
  157.7 0.4 convolution_convert_fusion
  158.1 0.9 fusion.10
  159.0 1.2 convolution_bitcast_fusion.1
  160.2 1.0 multiply_reduce_fusion.1
  161.3 0.0 copy-start.11
  161.3 1.1 fusion.1
  162.4 1.0 copy-done.6
  163.4 0.8 fusion.2
  164.2 1.9 pad_maximum_fusion
  166.1 0.0 reduce-scatter.10.cloned.1.call-update
  166.1 0.0 reduce-scatter.14.cloned.1.call-start
  166.2 1.4 convolution_bitcast_fusion.3
  167.6 5.1 copy.35
  172.6 2.9 copy.52
  175.5 0.0 reduce-scatter.14.cloned.1.call-update
  175.5 0.2 all-reduce.3.cloned.1.call-start
  175.8 2.0 fusion.54
  177.8 0.8 fusion.53
  178.7 42.9 %reduce-scatter.10.cloned.1.call-done = f32[1,192,2,1,128]{4,1,2,3,0:T(8,128)} async-done(((f32[1,3072,2,1,128]{4,1,2,3,0:T(8,128)}), f32[1,192,2,1,128]{4,1,2,3,0:T(8,128)}) %reduce-scatter.10.cloned.1.call-update) | async-done | bytes 196624 | tf_op jit(solution)/shard_map/reduce_scatter | solution.py:140
  221.5 1.0 fusion.42
  222.6 1.1 subtract_multiply_fusion
  223.7 0.1 copy.31
  223.8 0.0 copy-start.12
  223.8 3.0 convolution_bitcast_fusion.2
  226.8 0.0 all-reduce.3.cloned.1.call-update
  226.8 0.0 reduce-scatter.16.cloned.1.call-start
  226.9 2.6 fusion.67
  229.5 0.0 reduce-scatter.16.cloned.1.call-update
  229.5 0.0 reduce-scatter.12.cloned.1.call-start
  229.5 3.3 fusion.36
  232.9 0.0 reduce-scatter.12.cloned.1.call-update
  232.9 72.6 %reduce-scatter.14.cloned.1.call-done = f32[224,192]{1,0:T(8,128)} async-done(((f32[1792,192]{1,0:T(8,128)}), f32[224,192]{1,0:T(8,128)}) %reduce-scatter.14.cloned.1.call-update) | async-done | bytes 172048
  305.5 1.1 reshape_bitcast_fusion
  306.6 0.8 copy.36
  307.4 94.9 %all-reduce.3.cloned.1.call-done = f32[1,192,1792]{2,1,0:T(8,128)} async-done(((f32[1,192,1792]{2,1,0:T(8,128)}), f32[1,192,1792]{2,1,0:T(8,128)}) %all-reduce.3.cloned.1.call-update) | async-done | bytes 1376272 | tf_op jit(solution)/shard_map/psum | solution.py:158
  402.3 2.0 multiply_reduce_fusion
  404.3 1.8 fusion.34
  406.2 0.8 add_convert_fusion
  406.9 119.1 %reduce-scatter.16.cloned.1.call-done = f32[128,56]{0,1:T(8,128)} async-done(((f32[128,1792]{0,1:T(8,128)}), f32[128,56]{0,1:T(8,128)}) %reduce-scatter.16.cloned.1.call-update) | async-done | bytes 28688
  526.1 125.7 %reduce-scatter.12.cloned.1.call-done = f32[56,3,128]{2,0,1:T(8,128)} async-done(((f32[1792,3,128]{2,0,1:T(8,128)}), f32[56,3,128]{2,0,1:T(8,128)}) %reduce-scatter.12.cloned.1.call-update) | async-done | bytes 86032 | tf_op jit(solution)/shard_map/reduce_scatter | solution.py:151
  (52 shorter events, 0.2 us)
Async XLA Ops:
  7.2 150.5 %copy-start = (bf16[128,1792]{1,0:T(8,128)(2,1)S(1)}, bf16[128,1792]{1,0:T(8,128)(2,1)}, u32[]{:S(2)}) copy-start(bf16[128,1792]{1,0:T(8,128)(2,1)} %param.14) | copy-start | bytes 1376260
  7.2 214.4 %reduce-scatter.10.cloned.1.call-start = ((), (), s32[]{:S(2)}) async-start(), calls=%async_computation.4 | async-start | bytes 3342336 | tf_op jit(solution)/shard_map/reduce_scatter | solution.py:140
  7.2 98.2 %collective-permute-start = (bf16[1,150,3584]{2,1,0:T(8,128)(2,1)}, bf16[1,150,3584]{2,1,0:T(8,128)(2,1)}, u32[]{:S(2)}, u32[]{:S(2)}) collective-permute-start(bf16[1,150,3584]{2,1,0:T(8,128)(2,1)} %param.12), channel_id=1, source_target_pairs={{0,16},{16,32},{32,48},{48,64},{64,80},{80,96},{96,112},{112,128},... | collective-permute-start | bytes 3225608 | tf_op jit(solution)/shard_map/ppermute | solution.py:13
  62.9 42.2 %copy-start.15 = (s32[1,3072]{1,0:T(1,128)S(1)}, s32[1,3072]{1,0:T(1,128)}, u32[]{:S(2)}) copy-start(s32[1,3072]{1,0:T(1,128)} %param.18) | copy-start | bytes 36868
  62.9 42.5 %copy-start.20 = (s32[1,192]{1,0:T(1,128)S(1)}, s32[1,192]{1,0:T(1,128)}, u32[]{:S(2)}) copy-start(s32[1,192]{1,0:T(1,128)} %param.17) | copy-start | bytes 2308
  105.0 0.9 copy-start.2
  105.4 3.1 copy-start.13
  105.9 2.6 copy-start.3
  108.5 1.6 copy-start.1
  109.9 46.9 %copy-start.5 = (bf16[192,1792,1]{1,0,2:T(8,128)(2,1)}, bf16[192,1792,1]{1,0,2:T(8,128)(2,1)S(1)}, u32[]{:S(2)}) copy-start(bf16[192,1792,1]{1,0,2:T(8,128)(2,1)S(1)} %get-tuple-element.8) | copy-start | bytes 2064388
  109.9 29.9 %copy-start.19 = (f32[1,128]{1,0:T(1,128)S(1)}, f32[1,128]{1,0:T(1,128)}, u32[]{:S(2)}) copy-start(f32[1,128]{1,0:T(1,128)} %param.16) | copy-start | bytes 1540
  110.0 46.8 %copy-start.21 = (f32[1,128]{1,0:T(1,128)S(1)}, f32[1,128]{1,0:T(1,128)}, u32[]{:S(2)}) copy-start(f32[1,128]{1,0:T(1,128)} %param.15) | copy-start | bytes 1540
  110.8 46.9 %copy-start.17 = (f32[192]{0:T(256)}, f32[192]{0:T(256)S(1)}, u32[]{:S(2)}) copy-start(f32[192]{0:T(256)S(1)} %add_rsqrt_fusion) | copy-start | bytes 2308
  110.9 51.4 %copy-start.18 = (f32[192]{0:T(256)}, f32[192]{0:T(256)S(1)}, u32[]{:S(2)}) copy-start(f32[192]{0:T(256)S(1)} %add_rsqrt_fusion.1) | copy-start | bytes 2308
  139.8 17.9 %copy-start.4 = (bf16[1,192,1792]{2,1,0:T(8,128)(2,1)S(1)}, bf16[1,192,1792]{2,1,0:T(8,128)(2,1)}, u32[]{:S(2)}) copy-start(bf16[1,192,1792]{2,1,0:T(8,128)(2,1)} %copy.28) | copy-start | bytes 2064388
  156.8 1.2 copy-start.7
  159.0 1.2 copy-start.16
  161.3 4.9 copy-start.11
  162.4 1.0 copy-start.6
  166.1 139.4 %reduce-scatter.14.cloned.1.call-start = ((), (), s32[]{:S(2)}) async-start(), calls=%async_computation.7 | async-start | bytes 2064384
  172.6 3.1 copy-start.22
  175.5 226.8 %all-reduce.3.cloned.1.call-start = ((), (), s32[]{:S(2)}) async-start(), calls=%async_computation.5 | async-start | bytes 2752512 | tf_op jit(solution)/shard_map/psum | solution.py:158
  223.8 3.1 copy-start.12
  226.8 299.2 %reduce-scatter.16.cloned.1.call-start = ((), (), s32[]{:S(2)}) async-start(), calls=%async_computation.8 | async-start | bytes 946176
  229.5 422.3 %reduce-scatter.12.cloned.1.call-start = ((), (), s32[]{:S(2)}) async-start(), calls=%async_computation.6 | async-start | bytes 2838528 | tf_op jit(solution)/shard_map/reduce_scatter | solution.py:151
  232.9 169.4 %copy-start.14 = (f32[192]{0:T(256)S(1)}, f32[192]{0:T(256)}, u32[]{:S(2)}) copy-start(f32[192]{0:T(256)} %copy-done.13) | copy-start | bytes 2308
  307.4 96.9 %copy-start.9 = (bf16[1,192,224]{2,1,0:T(8,128)(2,1)S(1)}, bf16[1,192,224]{2,1,0:T(8,128)(2,1)}, u32[]{:S(2)}) copy-start(bf16[1,192,224]{2,1,0:T(8,128)(2,1)} %param.11) | copy-start | bytes 258052
  307.4 98.8 %copy-start.8 = (f32[1,192,224]{2,1,0:T(8,128)S(1)}, f32[1,192,224]{2,1,0:T(8,128)}, u32[]{:S(2)}) copy-start(f32[1,192,224]{2,1,0:T(8,128)} %copy.36) | copy-start | bytes 516100
  402.3 3.8 copy-start.10
Sparse Core Ops, SparseCore 0:
  166.2 55.2 reduce-scatter.9
  225.6 79.8 reduce-scatter.13
  308.1 94.1 all-reduce.2
  405.2 120.7 reduce-scatter.15
  529.0 122.6 reduce-scatter.11
where the time goes:
time: 659 us; the launch traced here: 658 us
  waiting for transfers between devices  455 us (69%)
  blocking collectives  125 us (19%)
  local copies, waits for them, and re-layouts  24.3 us (4%)
  matrix products  20.9 us (3%)
  between operations  14.8 us (2%)
  other arithmetic  12.2 us (2%)
    unnamed x7, waiting for transfers between devices  192 us
    reduce_scatter x1, waiting for transfers between devices, on_device(): lax.psum_scatter(grad_wqkv, ('seq', 'dp'), scatter_dimension=0, tiled=True)  126 us
    psum x1, waiting for transfers between devices, on_device(): grad_full = lax.psum(grad_hidden, 'mp')  94.9 us
    reduce_scatter x1, waiting for transfers between devices, on_device(): lax.psum_scatter(key_terms, 'seq', scatter_dimension=1, tiled=True)  42.9 us
    all_gather x1, blocking collectives, on_device(): lax.all_gather(grad_out, 'mp', axis=2, tiled=True)  41.4 us
    all_gather x1, blocking collectives, on_device(): lax.all_gather(latents, 'mp', axis=2, tiled=True)  38.2 us
    all_gather x1, blocking collectives, on_device(): value_piece = lax.all_gather(values, 'seq', axis=1, tiled=True)  28.8 us
    all_gather x1, blocking collectives, on_device(): key_piece = lax.all_gather(key_norm, 'seq', axis=1, tiled=True)  17 us
  transfers between devices with their start and end apart: 6, of which 5 were waited for; matrix products, arithmetic and copies ran while one was open for 6% of the time, Pallas kernels for 0%

commit v1 on v0

v1 whole, which is shorter than its diff:
```python
import functools

import jax
import jax.numpy as jnp
from jax import lax
from jax.experimental import pallas as pl
from jax.experimental.pallas import tpu as pltpu
from jax.sharding import PartitionSpec as P

EPSILON = 1e-06
NEG_FILL = -1e30
TAIL = 48

F32 = jnp.float32
BF16 = jnp.bfloat16
MESH = pl.DeviceIdType.MESH


def dot_nn(a, b):
    return lax.dot_general(a, b, (((1,), (0,)), ((), ())), preferred_element_type=F32)


def dot_nt(a, b):
    return lax.dot_general(a, b, (((1,), (1,)), ((), ())), preferred_element_type=F32)


def dot_tn(a, b):
    return lax.dot_general(a, b, (((0,), (0,)), ((), ())), preferred_element_type=F32)


def norm_back(raw, inv_norm, gains, upstream):
    inner_dot = jnp.mean(upstream * gains * raw, axis=-1, keepdims=True)
    return inv_norm * (gains * upstream - raw * inv_norm * inv_norm * inner_dot)


def send(src, dst, send_sem, recv_sem, where):
    pltpu.make_async_remote_copy(
        src_ref=src, dst_ref=dst, send_sem=send_sem, recv_sem=recv_sem,
        device_id=where, device_id_type=MESH,
    ).start()


def arrived(dst, send_sem, recv_sem, where):
    pltpu.make_async_remote_copy(
        src_ref=dst, dst_ref=dst, send_sem=send_sem, recv_sem=recv_sem,
        device_id=where, device_id_type=MESH,
    ).wait_recv()


def drained(src, send_sem, recv_sem, where):
    pltpu.make_async_remote_copy(
        src_ref=src, dst_ref=src, send_sem=send_sem, recv_sem=recv_sem,
        device_id=where, device_id_type=MESH,
    ).wait_send()


def block_kernel(
    sizes,
    lat_ref, go_ref, win_ref, tail_ref, wq_ref, wo_ref, qg_ref, kg_ref, frame_ref, group_ref, len_ref,
    mixed_ref, gl_ref, gwq_ref, gwo_ref,
    prev, ga_all, hid_all, ssq_all, kv_all, qo_all, p_all, stats_all, ho_all, wo_recv,
    gh_send, gh_recv, dot_all, cx_send, cx_recv, half, dx_send, dx_recv, quarter, zs_send, zs_recv,
    proj, scale_s, gate_s, normed_s, go_acc, mx_s, rs_s, acc_s, dk_s, dv_s, gw_s,
    prev_sem, ga_ss, ga_rs, hid_ss, hid_rs, ssq_ss, ssq_rs, kv_ss, kv_fs, kv_rs, qo_ss, qo_fs, qo_rs,
    st_ss, st_rs, ho_ss, ho_rs, wo_ss, wo_rs, gh_ss, gh_rs, dot_ss, dot_rs, cx_ss, cx_rs, dx_ss, dx_rs,
    zs_ss, zs_rs,
):
    S, M, frames = sizes
    Z = S // 2
    rows, width = lat_ref.shape
    hd = qg_ref.shape[1]
    factor = hd ** (-0.5)
    piece = width // 4
    s = lax.axis_index("seq")
    m = lax.axis_index("mp")
    d = lax.axis_index("dp")
    z, c = lax.div(s, 2), lax.rem(s, 2)
    mate = z * 2 + 1 - c
    other_d = 1 - d

    barrier = pltpu.get_barrier_semaphore()
    for k in range(1, M):
        pl.semaphore_signal(barrier, inc=1, device_id={"mp": lax.rem(m + k, M)}, device_id_type=MESH)
    for k in range(1, S):
        pl.semaphore_signal(barrier, inc=1, device_id={"seq": lax.rem(s + k, S)}, device_id_type=MESH)
    pl.semaphore_signal(barrier, inc=1, device_id={"dp": other_d}, device_id_type=MESH)

    eye = lax.broadcasted_iota(jnp.int32, (rows, rows), 0) == lax.broadcasted_iota(jnp.int32, (rows, rows), 1)

    def to_row(col):
        return jnp.sum(jnp.where(eye, jnp.broadcast_to(col, (rows, rows)), 0.0), axis=0, keepdims=True)

    def to_col(row):
        return jnp.sum(jnp.where(eye, jnp.broadcast_to(row, (rows, rows)), 0.0), axis=1, keepdims=True)

    lat = lat_ref[...].astype(F32)
    ssq = to_row(jnp.sum(lat * lat, axis=1, keepdims=True))
    ssq_all[m] = jnp.broadcast_to(ssq, (8, rows))
    local_frame = frame_ref[...] - frames * s
    own_rows = win_ref.shape[0]
    pick_own = jnp.where(
        lax.broadcasted_iota(jnp.int32, (own_rows, rows), 0) == local_frame, 1.0, 0.0
    ).astype(BF16)
    pick_prev = jnp.where(
        lax.broadcasted_iota(jnp.int32, (TAIL, rows), 0) == local_frame + TAIL, 1.0, 0.0
    ).astype(BF16)
    mod_own = dot_tn(pick_own, win_ref[...])

    pl.semaphore_wait(barrier, (M - 1) + (S - 1) + 1)

    after = {"seq": lax.rem(s + 1, S)}
    send(tail_ref, prev, prev_sem.at[0], prev_sem.at[1], after)
    for k in range(1, M):
        to = lax.rem(m + k, M)
        send(ssq_all.at[m], ssq_all.at[m], ssq_ss.at[to], ssq_rs.at[m], {"mp": to})

    arrived(prev, prev_sem.at[0], prev_sem.at[1], after)
    modulation = mod_own + dot_tn(pick_prev, prev[...])
    scale = modulation[:, :width]
    gate = modulation[:, 256:256 + width]
    scale_s[...] = scale
    gate_s[...] = gate
    ga_all[m] = (go_ref[...].astype(F32) * gate).astype(BF16)
    for k in range(1, M):
        to = lax.rem(m + k, M)
        send(ga_all.at[m], ga_all.at[m], ga_ss.at[to], ga_rs.at[m], {"mp": to})

    for k in range(1, M):
        at = lax.rem(m + k, M)
        arrived(ssq_all.at[at], ssq_ss.at[at], ssq_rs.at[at], {"mp": at})
    total = ssq_all[0, 0:1, :]
    for k in range(1, M):
        total = total + ssq_all[k, 0:1, :]
    inv_col = to_col(lax.rsqrt(total * (1.0 / (M * width)) + EPSILON))
    normed = lat * inv_col
    normed_s[...] = normed
    hid_all[m] = (normed * (1.0 + scale)).astype(BF16)
    for k in range(1, M):
        to = lax.rem(m + k, M)
        send(hid_all.at[m], hid_all.at[m], hid_ss.at[to], hid_rs.at[m], {"mp": to})
    for k in range(1, M):
        to = lax.rem(m + k, M)
        send(wo_ref.at[to], wo_recv.at[m], wo_ss.at[to], wo_rs.at[m], {"mp": to})
    wo_recv[m] = wo_ref[m]

    go_acc[...] = dot_nt(ga_all[m], wo_ref[m])

    def take_ga(k, carry):
        at = lax.rem(m + k, M)
        arrived(ga_all.at[at], ga_ss.at[at], ga_rs.at[at], {"mp": at})
        go_acc[...] += dot_nt(ga_all[at], wo_ref[at])
        return carry

    lax.fori_loop(1, M, take_ga, 0)
    proj[...] = dot_nn(hid_all[m], wq_ref[m])

    def take_hid(k, carry):
        at = lax.rem(m + k, M)
        arrived(hid_all.at[at], hid_ss.at[at], hid_rs.at[at], {"mp": at})
        proj[...] += dot_nn(hid_all[at], wq_ref[at])
        return carry

    lax.fori_loop(1, M, take_hid, 0)
    q_gain, k_gain = qg_ref[...], kg_ref[...]
    query_raw, key_raw = proj[:, :hd], proj[:, hd:2 * hd]
    query_inv = lax.rsqrt(jnp.mean(query_raw * query_raw, axis=-1, keepdims=True) + EPSILON)
    key_inv = lax.rsqrt(jnp.mean(key_raw * key_raw, axis=-1, keepdims=True) + EPSILON)
    kv_all[s, :, :hd] = (key_raw * key_inv * k_gain).astype(BF16)
    kv_all[s, :, hd:] = proj[:, 2 * hd:].astype(BF16)
    qo_all[s, :, :hd] = (query_raw * query_inv * q_gain).astype(BF16)
    qo_all[s, :, hd:] = go_acc[...].astype(BF16)

    def kv_to(t):
        send(kv_all.at[s], kv_all.at[s], kv_ss.at[t], kv_rs.at[s], {"seq": t})

    def qo_to(t):
        send(qo_all.at[s], qo_all.at[s], qo_ss.at[t], qo_rs.at[s], {"seq": t})

    kv_bound = (c == 0) & (z > 0)
    qo_bound = (c == 1) & (z < Z - 1)
    kv_to(mate)
    qo_to(mate)
    for k in range(1, Z):
        @pl.when(z + k < Z)
        def _():
            kv_to(s + 2 * k)

        @pl.when(z - k >= 0)
        def _():
            qo_to(s - 2 * k)

        if k == 1:
            @pl.when(kv_bound)
            def _():
                kv_to(s - 1)

            @pl.when(qo_bound)
            def _():
                qo_to(s + 1)

    own_group = to_col(group_ref[s].astype(F32))
    clip_length = len_ref[0]
    query = qo_all[s, :, :hd]
    upstream = qo_all[s, :, hd:]
    mx_s[...] = jnp.full_like(mx_s, NEG_FILL)

    def score(t):
        key_place = t * rows + lax.broadcasted_iota(jnp.int32, (1, rows), 1)
        allowed = (group_ref[t].astype(F32) <= own_group) & (key_place < clip_length)
        logits = dot_nt(qo_all[s, :, :hd], kv_all[t, :, :hd]) * factor
        logits = jnp.where(allowed, logits, NEG_FILL)
        p_all[t] = logits
        mx_s[...] = jnp.maximum(mx_s[...], jnp.max(logits, axis=-1, keepdims=True))

    def wait_kv(t):
        arrived(kv_all.at[t], kv_fs.at[t], kv_rs.at[t], {"seq": mate})

    def wait_qo(t):
        arrived(qo_all.at[t], qo_fs.at[t], qo_rs.at[t], {"seq": mate})

    score(s)
    wait_kv(mate)
    score(mate)

    def take_direct(k, carry):
        @pl.when(z - k >= 0)
        def _():
            t = s - 2 * k
            wait_kv(t)
            send(kv_all.at[t], kv_all.at[t], kv_fs.at[t], kv_rs.at[t], {"seq": mate})

        @pl.when(z + k < Z)
        def _():
            t = s + 2 * k
            wait_qo(t)
            send(qo_all.at[t], qo_all.at[t], qo_fs.at[t], qo_rs.at[t], {"seq": mate})

        @pl.when(z - k >= 0)
        def _():
            score(s - 2 * k)

        return carry

    lax.fori_loop(1, Z, take_direct, 0)

    @pl.when(qo_bound)
    def _():
        wait_kv(s + 1)
        score(s + 1)

    def take_mate(k, carry):
        @pl.when(z - k >= 0)
        def _():
            t = mate - 2 * k
            wait_kv(t)
            score(t)

        return carry

    lax.fori_loop(1, Z, take_mate, 0)

    last = jnp.minimum(s + 2, S)
    rs_s[...] = jnp.zeros_like(rs_s)
    acc_s[...] = jnp.zeros_like(acc_s)

    def forward(t, carry):
        unnorm = jnp.exp(p_all[t] - mx_s[...])
        p_all[t] = unnorm
        rs_s[...] += jnp.sum(unnorm, axis=-1, keepdims=True)
        acc_s[...] += dot_nn(unnorm.astype(BF16), kv_all[t, :, hd:])
        return carry

    lax.fori_loop(0, last, forward, 0)
    inv_sum = 1.0 / rs_s[...]
    heads_out = (acc_s[...] / rs_s[...]).astype(BF16)
    ho_all[m] = heads_out
    out_dot = jnp.sum(upstream.astype(F32) * heads_out.astype(F32), axis=-1, keepdims=True)
    stats_all[s] = jnp.concatenate(
        [to_row(mx_s[...]), to_row(inv_sum), to_row(out_dot), jnp.zeros((5, rows), F32)], axis=0
    )
    for t in range(S):
        @pl.when((t <= s + 1) & (t != s))
        def _():
            send(stats_all.at[s], stats_all.at[s], st_ss.at[t], st_rs.at[s], {"seq": jnp.int32(t)})
    for k in range(1, M):
        to = lax.rem(m + k, M)
        send(ho_all.at[m], ho_all.at[m], ho_ss.at[to], ho_rs.at[m], {"mp": to})

    acc_s[...] = jnp.zeros_like(acc_s)

    def back_query(t, carry):
        probs = p_all[t] * inv_sum
        grad_probs = dot_nt(upstream, kv_all[t, :, hd:])
        grad_logits = (probs * (grad_probs - out_dot)).astype(BF16)
        acc_s[...] += dot_nn(grad_logits, kv_all[t, :, :hd])
        return carry

    lax.fori_loop(0, last, back_query, 0)

    dk_s[...] = jnp.zeros_like(dk_s)
    dv_s[...] = jnp.zeros_like(dv_s)
    own_place = s * rows + lax.broadcasted_iota(jnp.int32, (rows, 1), 0)

    def back_key(t, carry):
        @pl.when((t != s) & jnp.logical_not((lax.rem(t, 2) == c) & (lax.div(t, 2) > z)))
        def _():
            wait_qo(t)

        @pl.when(t != s)
        def _():
            arrived(stats_all.at[t], st_ss.at[t], st_rs.at[t], {"seq": t})

        stats = stats_all[t]
        allowed = (own_group <= group_ref[t].astype(F32)) & (own_place < clip_length)
        logits = dot_nt(kv_all[s, :, :hd], qo_all[t, :, :hd]) * factor
        probs = jnp.exp(jnp.where(allowed, logits, NEG_FILL) - stats[0:1]) * stats[1:2]
        grad_probs = dot_nt(kv_all[s, :, hd:], qo_all[t, :, hd:])
        grad_logits = (probs * (grad_probs - stats[2:3])).astype(BF16)
        dk_s[...] += dot_nn(grad_logits, qo_all[t, :, :hd])
        dv_s[...] += dot_nn(probs.astype(BF16), qo_all[t, :, hd:])
        return carry

    lax.fori_loop(jnp.maximum(s - 1, 0), S, back_key, 0)
    grad_query = norm_back(query_raw, query_inv, q_gain, acc_s[...] * factor)
    grad_key = norm_back(key_raw, key_inv, k_gain, dk_s[...] * factor)
    grad_proj = jnp.concatenate([grad_query, grad_key, dv_s[...]], axis=1).astype(BF16)

    def give_gh(k, carry):
        to = lax.rem(m + k, M)
        gh_send[to] = dot_nt(grad_proj, wq_ref[to]).astype(BF16)
        send(gh_send.at[to], gh_recv.at[m], gh_ss.at[to], gh_rs.at[m], {"mp": to})
        return carry

    lax.fori_loop(1, M, give_gh, 0)

    mine = pl.multiple_of(c * 2 * piece, 8)
    theirs = pl.multiple_of((1 - c) * 2 * piece, 8)

    def give_core(k, carry):
        at = lax.rem(z + k, Z)
        gw_s[:, :3 * hd] = dot_tn(hid_all[at], grad_proj)
        gw_s[:, 3 * hd:] = dot_tn(ga_all[at], heads_out)
        half[at] = gw_s[pl.ds(mine, 2 * piece), :]
        cx_send[at] = gw_s[pl.ds(theirs, 2 * piece), :].astype(BF16)
        send(cx_send.at[at], cx_recv.at[at], cx_ss.at[at], cx_rs.at[at], {"seq": mate})
        return carry

    lax.fori_loop(1, Z + 1, give_core, 0)

    def give_clip(k, carry):
        at = lax.rem(z + k, Z)
        arrived(cx_recv.at[at], cx_ss.at[at], cx_rs.at[at], {"seq": mate})
        both = half[at] + cx_recv[at].astype(F32)
        first, second = both[:piece], both[piece:]
        quarter[at] = jnp.where(d == 0, first, second)
        dx_send[at] = jnp.where(d == 0, second, first).astype(BF16)
        send(dx_send.at[at], dx_recv.at[at], dx_ss.at[at], dx_rs.at[at], {"dp": other_d})
        return carry

    lax.fori_loop(1, Z + 1, give_clip, 0)

    def give_z(k, carry):
        at = lax.rem(z + k, Z)
        arrived(dx_recv.at[at], dx_ss.at[at], dx_rs.at[at], {"dp": other_d})
        both = quarter[at] + dx_recv[at].astype(F32)
        quarter[at] = both

        @pl.when(k < Z)
        def _():
            zs_send[at] = both.astype(BF16)
            send(zs_send.at[at], zs_recv.at[z], zs_ss.at[at], zs_rs.at[z], {"seq": at * 2 + c})

        return carry

    lax.fori_loop(1, Z + 1, give_z, 0)

    acc_mixed = dot_nn(ho_all[m], wo_recv[m])
    go_mixed = acc_mixed
    for k in range(1, M):
        at = lax.rem(m + k, M)
        arrived(ho_all.at[at], ho_ss.at[at], ho_rs.at[at], {"mp": at})
        arrived(wo_recv.at[at], wo_ss.at[at], wo_rs.at[at], {"mp": at})
        go_mixed = go_mixed + dot_nn(ho_all[at], wo_recv[at])
    mixed_ref[...] = (lat_ref[...].astype(F32) + gate_s[...] * go_mixed).astype(BF16)

    grad_full = dot_nt(grad_proj, wq_ref[m])
    for k in range(1, M):
        at = lax.rem(m + k, M)
        arrived(gh_recv.at[at], gh_ss.at[at], gh_rs.at[at], {"mp": at})
        grad_full = grad_full + gh_recv[at].astype(F32)
    grad_normed = grad_full * (1.0 + scale_s[...])
    inner = to_row(jnp.sum(grad_normed * normed_s[...], axis=1, keepdims=True))
    dot_all[m] = jnp.broadcast_to(inner, (8, rows))
    for k in range(1, M):
        to = lax.rem(m + k, M)
        send(dot_all.at[m], dot_all.at[m], dot_ss.at[to], dot_rs.at[m], {"mp": to})

    weight = quarter[z]
    for k in range(1, Z):
        at = lax.rem(z + k, Z)
        arrived(zs_recv.at[at], zs_ss.at[at], zs_rs.at[at], {"seq": at * 2 + c})
        weight = weight + zs_recv[at].astype(F32)
    gwq_ref[...] = weight[:, :3 * hd]
    gwo_ref[...] = weight[:, 3 * hd:]

    for k in range(1, M):
        at = lax.rem(m + k, M)
        arrived(dot_all.at[at], dot_ss.at[at], dot_rs.at[at], {"mp": at})
    total = dot_all[0, 0:1, :]
    for k in range(1, M):
        total = total + dot_all[k, 0:1, :]
    mean_col = to_col(total * (1.0 / (M * width)))
    grad_inputs = inv_col * (grad_normed - normed_s[...] * mean_col)
    gl_ref[...] = (go_ref[...].astype(F32) + grad_inputs).astype(BF16)

    drained(tail_ref, prev_sem.at[0], prev_sem.at[1], after)

    def drain_mp(k, carry):
        to = lax.rem(m + k, M)
        there = {"mp": to}
        drained(ssq_all.at[m], ssq_ss.at[to], ssq_rs.at[m], there)
        drained(ga_all.at[m], ga_ss.at[to], ga_rs.at[m], there)
        drained(hid_all.at[m], hid_ss.at[to], hid_rs.at[m], there)
        drained(wo_ref.at[to], wo_ss.at[to], wo_rs.at[m], there)
        drained(ho_all.at[m], ho_ss.at[to], ho_rs.at[m], there)
        drained(gh_send.at[to], gh_ss.at[to], gh_rs.at[m], there)
        drained(dot_all.at[m], dot_ss.at[to], dot_rs.at[m], there)
        return carry

    lax.fori_loop(1, M, drain_mp, 0)

    def kv_left(t):
        drained(kv_all.at[s], kv_ss.at[t], kv_rs.at[s], {"seq": t})

    def qo_left(t):
        drained(qo_all.at[s], qo_ss.at[t], qo_rs.at[s], {"seq": t})

    kv_left(mate)
    qo_left(mate)

    @pl.when(kv_bound)
    def _():
        kv_left(s - 1)

    @pl.when(qo_bound)
    def _():
        qo_left(s + 1)

    def drain_seq(k, carry):
        @pl.when(z + k < Z)
        def _():
            t = s + 2 * k
            kv_left(t)
            drained(qo_all.at[t], qo_fs.at[t], qo_rs.at[t], {"seq": mate})

        @pl.when(z - k >= 0)
        def _():
            t = s - 2 * k
            qo_left(t)
            drained(kv_all.at[t], kv_fs.at[t], kv_rs.at[t], {"seq": mate})

        at = lax.rem(z + k, Z)
        drained(zs_send.at[at], zs_ss.at[at], zs_rs.at[z], {"seq": at * 2 + c})
        return carry

    lax.fori_loop(1, Z, drain_seq, 0)

    def drain_weights(at, carry):
        drained(cx_send.at[at], cx_ss.at[at], cx_rs.at[at], {"seq": mate})
        drained(dx_send.at[at], dx_ss.at[at], dx_rs.at[at], {"dp": other_d})
        return carry

    lax.fori_loop(0, Z, drain_weights, 0)

    def drain_stats(t, carry):
        @pl.when(t != s)
        def _():
            drained(stats_all.at[s], st_ss.at[t], st_rs.at[s], {"seq": t})

        return carry

    lax.fori_loop(0, last, drain_stats, 0)


def on_device(S, M, latents, grad_out, sync_mod, w_qkv, w_out, q_gain, k_gain, frame_of, group_id, clip_len):
    _, rows, width = latents.shape
    frames = sync_mod.shape[1]
    model_width = sync_mod.shape[2] // 2
    hd = q_gain.shape[1]
    Z = S // 2
    piece = width // 4
    m = lax.axis_index("mp")
    scale_cols = lax.dynamic_slice(sync_mod[0], (0, m * width), (frames, width))
    gate_cols = lax.dynamic_slice(sync_mod[0], (0, model_width + m * width), (frames, width))
    own_rows = -(-frames // 16) * 16
    side = 256 - width
    window = jnp.concatenate(
        [jnp.pad(scale_cols, ((0, 0), (0, side))), jnp.pad(gate_cols, ((0, 0), (0, side)))], axis=1
    )
    tail = window[frames - TAIL:]
    window = jnp.pad(window, ((0, own_rows - frames), (0, 0)))
    wq_parts = w_qkv.reshape(M, width, 3 * hd)
    wo_parts = jnp.transpose(w_out.reshape(hd, M, width), (1, 0, 2))
    vmem = pl.BlockSpec(memory_space=pltpu.VMEM)

    def buf(shape, dtype=BF16):
        return pltpu.VMEM(shape, dtype)

    def sems(*counts):
        return [pltpu.SemaphoreType.DMA((n,)) for n in counts]

    scratch = [
        buf((TAIL, 512)), buf((M, rows, width)), buf((M, rows, width)), buf((M, 8, rows), F32),
        buf((S, rows, 2 * hd)), buf((S, rows, 2 * hd)), buf((S, rows, rows), F32), buf((S, 8, rows), F32),
        buf((M, rows, hd)), buf((M, hd, width)),
        buf((M, rows, width)), buf((M, rows, width)), buf((M, 8, rows), F32),
        buf((Z, 2 * piece, 4 * hd)), buf((Z, 2 * piece, 4 * hd)), buf((Z, 2 * piece, 4 * hd), F32),
        buf((Z, piece, 4 * hd)), buf((Z, piece, 4 * hd)), buf((Z, piece, 4 * hd), F32),
        buf((Z, piece, 4 * hd)), buf((Z, piece, 4 * hd)),
        buf((rows, 3 * hd), F32), buf((rows, width), F32), buf((rows, width), F32), buf((rows, width), F32),
        buf((rows, hd), F32), buf((rows, 1), F32), buf((rows, 1), F32), buf((rows, hd), F32),
        buf((rows, hd), F32), buf((rows, hd), F32), buf((width, 4 * hd), F32),
    ] + sems(2, M, M, M, M, M, M, S, S, S, S, S, S, S, S, M, M, M, M, M, M, M, M, Z, Z, Z, Z, Z, Z)
    mixed, grad_latents, grad_wqkv, grad_wout = pl.pallas_call(
        functools.partial(block_kernel, (S, M, frames)),
        out_shape=(
            jax.ShapeDtypeStruct((rows, width), BF16),
            jax.ShapeDtypeStruct((rows, width), BF16),
            jax.ShapeDtypeStruct((piece, 3 * hd), F32),
            jax.ShapeDtypeStruct((piece, hd), F32),
        ),
        in_specs=[vmem] * 10 + [pl.BlockSpec(memory_space=pltpu.SMEM)],
        out_specs=(vmem, vmem, vmem, vmem),
        scratch_shapes=scratch,
        compiler_params=pltpu.CompilerParams(
            collective_id=0, has_side_effects=True, vmem_limit_bytes=60 * 1024 * 1024
        ),
    )(
        latents[0], grad_out[0], window, tail, wq_parts, wo_parts, q_gain, k_gain, frame_of,
        group_id.reshape(S, 1, rows), clip_len,
    )
    return (
        mixed[None], grad_latents[None], grad_wqkv.reshape(piece, 3, hd), jnp.transpose(grad_wout),
    )


def solution(mesh):
    in_specs = (
        P("dp", "seq", "mp"),
        P("dp", "seq", "mp"),
        P("dp", "seq", None),
        P(None, None, "mp"),
        P("mp", None),
        P("mp", None),
        P("mp", None),
        P("dp", "seq"),
        P("dp", None),
        P("dp"),
    )
    out_specs = (
        P("dp", "seq", "mp"),
        P("dp", "seq", "mp"),
        P(("seq", "dp"), None, "mp"),
        P("mp", ("seq", "dp")),
    )
    return jax.shard_map(
        functools.partial(on_device, mesh.shape["seq"], mesh.shape["mp"]),
        mesh=mesh, in_specs=in_specs, out_specs=out_specs, check_vma=False,
    )
```

time: 659 us -> 121 us (0.18)
  waiting for transfers between devices: 455 us -> 0 us
  blocking collectives: 125 us -> 0 us
  Pallas kernels: 0 us -> 97.4 us
  matrix products: 20.9 us -> 0 us
  between operations: 14.8 us -> 1.34 us
  other arithmetic: 12.2 us -> 0.7 us
    unnamed x7 -> x0, waiting for transfers between devices: 192 us -> none
    reduce_scatter x2 -> x0, waiting for transfers between devices: 169 us -> none  [the longest x1 126 us: on_device(): lax.psum_scatter(grad_wqkv, ('seq', 'dp'), scatter_dimension=0, tiled=True)]
    all_gather x4 -> x0, blocking collectives: 125 us -> none  [the longest x1 41.4 us: on_device(): lax.all_gather(grad_out, 'mp', axis=2, tiled=True)]
    pallas_call x0 -> x1, Pallas kernels: none -> 97.4 us  [on_device(): pl.pallas_call(functools.partial(block_kernel, (S, M, frames)), out_shape...]
    psum x1 -> x0, waiting for transfers between devices: 94.9 us -> none  [on_device(): grad_full = lax.psum(grad_hidden, 'mp')]
    dot_general x13 -> x0, matrix products: 20.9 us -> none  [the longest x1 3.34 us: on_device(): jnp.einsum('te,tf->ef', flat_hidden, grad_proj, preferred_element_type=jn...]
    reshape x0 -> x4, local copies, waits for them, and re-layouts: none -> 12.3 us  [the longest x2 10.6 us: on_device(): wq_parts = w_qkv.reshape(M, width, 3 * hd)]
    unnamed x53 -> x10, local copies, waits for them, and re-layouts: 16.3 us -> 6.74 us
  transfers between devices with their start and end apart: 6 -> 0, of which waited for: 5 -> 0; matrix products, arithmetic and copies ran while one was open for 6% -> 0% of each run, Pallas kernels for 0% -> 0%
where the time goes in v1:
time: 121 us
  Pallas kernels  97.4 us (80%)
  local copies, waits for them, and re-layouts  21.4 us (18%)
  between operations  1.34 us (1%)
    pallas_call x1, Pallas kernels, on_device(): pl.pallas_call(functools.partial(block_kernel, (S, M, frames)), out_shape...  97.4 us
    reshape x2, local copies, waits for them, and re-layouts, on_device(): wq_parts = w_qkv.reshape(M, width, 3 * hd)  10.6 us
    unnamed x10, local copies, waits for them, and re-layouts  6.74 us

profile of v1, /device:TPU:1, one launch (start us, length us, event | category | flops | bytes accessed | tf_op | source)
XLA Modules:
  0.0 120.8 jit_solution(1690030884693094811)
XLA Ops:
  0.6 1.1 dynamic-slice_bitcast_fusion.1
  1.8 0.7 pad.13.win_ref
  2.4 0.6 slice.4.tail_ref
  3.1 8.2 %copy.21 = bf16[1792,3,128]{2,1,0:T(4,128)(2,1)S(1)} copy(bf16[1792,3,128]{2,0,1:T(8,128)(2,1)} %param.13) | data formatting | bytes 2752512 | tf_op jit(solution)/shard_map/reshape | solution.py:502
  11.3 0.0 copy-start
  11.3 2.4 %reshape.26.wq_ref = bf16[8,224,384]{2,1,0:T(8,128)(2,1)} reshape(bf16[1792,3,128]{2,1,0:T(4,128)(2,1)S(1)} %copy.21) | data formatting | bytes 2752512 | tf_op jit(solution)/shard_map/reshape | solution.py:502
  13.7 0.0 copy-done
  13.7 0.0 copy-start.1
  13.7 0.3 copy.17
  13.9 1.0 copy.18
  14.9 0.5 broadcast.15
  15.5 0.0 copy-done.1
  15.5 0.7 reduce.3
  16.1 0.7 reshape.24.group_ref
  17.5 97.4 %shard_map.129 = (bf16[192,224]{1,0:T(8,128)(2,1)}, bf16[192,224]{1,0:T(8,128)(2,1)}, f32[56,384]{1,0:T(8,128)}, f32[56,128]{1,0:T(8,128)}) custom-call(bf16[192,224]{1,0:T(8,128)(2,1)} %bitcast.18, bf16[192,224]{1,0:T(8,128)(2,1)} %bitcast.19, bf16[160,512]{1,0:T(8,128)(2,1)} %pad.13.win_ref, bf16[48,512]{1,0:T(8,128)(2,1)} %slice.4.tail_ref, ...), custom_call_target="tpu_custom_call" | custom-call | tf_op jit(solution)/shard_map/pallas_call | solution.py:524
  114.9 1.5 %copy_bitcast_fusion = f32[56,3,128]{2,0,1:T(8,128)} fusion(f32[56,384]{1,0:T(8,128)} %get-tuple-element.10), kind=kLoop, calls=%fused_computation.5 | loop fusion | bytes 172032
  116.4 1.5 %copy.29 = bf16[1,192,224]{2,1,0:T(8,128)(2,1)} copy(bf16[1,192,224]{2,1,0:T(8,128)(2,1)} %bitcast.21) | data formatting | bytes 172032
  117.9 1.5 %copy.30 = bf16[1,192,224]{2,1,0:T(8,128)(2,1)} copy(bf16[1,192,224]{2,1,0:T(8,128)(2,1)} %bitcast.20) | data formatting | bytes 172032
  119.5 1.4 %copy.31 = f32[128,56]{0,1:T(8,128)} copy(f32[128,56]{0,1:T(8,128)} %bitcast.22) | data formatting | bytes 57344
  (1 shorter events, 0.0 us)
Async XLA Ops:
  11.3 2.4 %copy-start = (bf16[128,1792]{1,0:T(8,128)(2,1)S(1)}, bf16[128,1792]{1,0:T(8,128)(2,1)}, u32[]{:S(2)}) copy-start(bf16[128,1792]{1,0:T(8,128)(2,1)} %param.14) | copy-start | bytes 1376260
  13.7 1.8 %copy-start.1 = (s32[1,3072]{1,0:T(1,128)S(1)}, s32[1,3072]{1,0:T(1,128)}, u32[]{:S(2)}) copy-start(s32[1,3072]{1,0:T(1,128)} %param.18) | copy-start | bytes 36868
